TPU v7x, 512 devices: a whole 4x4x16 slice. The times are simulated.
512 devices in a mesh: aux: 8 (over z_hi, core), pair: 64 (over z_lo, y, x).
Axes of the slice: x: 4, y: 4, z: 16 (z_hi: 4, z_lo: 4; z = z_hi * 4 + z_lo), core: 2. Of those that a mesh axis runs over, the one named last changes fastest.
Arguments:
- metric_factor: bfloat16 [16384, 16384], P('pair', 'aux'), as said below
- three_centre: bfloat16 [16384, 1536], P('aux', 'pair')
- occ_energy: float32 [2], replicated, may hold values from -2 to -0.3
- virt_energy: float32 [768], replicated, may hold values from 0.2 to 3
Outputs:
- amplitudes: float32 [1536, 1536], P('pair', 'aux')
- energy: float32 [], replicated
Inputs may be any that keep to these rules, and one draw needn't show every extreme that they name: metric_factor is lower triangular: every entry above the diagonal is zero, and its diagonal lies between 0.5 and 1.5.
All inputs are finite; a program needn't handle non-finite values.
Results may differ from a plain program's by a relative error of at most 0.0023.
Values may be sent and summed in bfloat16 or wider, within the bound.
A program may use at most 64 MiB of HBM per device.

v0:
```python
import jax
import jax.numpy as jnp
from jax import lax
from jax.sharding import PartitionSpec as P


def shards(metric_factor, three_centre, occ_energy, virt_energy):
    aux_count = lax.axis_size("aux")
    pair_count = lax.axis_size("pair")
    aux_id = lax.axis_index("aux")
    pair_id = lax.axis_index("pair")
    pairs_total = three_centre.shape[1] * pair_count
    share_cols = pairs_total // aux_count
    share_rows = pairs_total // pair_count
    partial_fit = jnp.dot(
        metric_factor,
        lax.all_gather(three_centre, "pair", axis=1, tiled=True),
        preferred_element_type=jnp.float32,
    )
    own_share = lax.psum_scatter(partial_fit, "aux", scatter_dimension=1, tiled=True).astype(
        jnp.bfloat16
    )
    fitted = lax.all_gather(own_share, "aux", axis=1, tiled=True)
    integrals = lax.psum_scatter(
        lax.dot_general(
            fitted, own_share, (((0,), (0,)), ((), ())), preferred_element_type=jnp.float32
        ),
        "pair",
        scatter_dimension=0,
        tiled=True,
    )
    pair_gap = (virt_energy[None, :] - occ_energy[:, None]).reshape(-1)
    row_gap = lax.dynamic_slice_in_dim(pair_gap, pair_id * share_rows, share_rows, 0)
    col_gap = lax.dynamic_slice_in_dim(pair_gap, aux_id * share_cols, share_cols, 0)
    denominator = row_gap[:, None] + col_gap[None, :]
    amplitudes = integrals / denominator
    local_energy = jnp.sum(integrals * amplitudes)
    energy = -lax.psum(local_energy, ("aux", "pair"))
    return (amplitudes, energy)


def solution(mesh):
    in_specs = (P("pair", "aux"), P("aux", "pair"), P(), P())
    out_specs = (P("pair", "aux"), P())
    return jax.shard_map(shards, mesh=mesh, in_specs=in_specs, out_specs=out_specs, check_vma=False)
```

profile of v0, /device:TPU:1, one launch (start us, length us, event | category | flops | bytes accessed | tf_op | source)
XLA Modules:
  0.0 956.0 jit_solution(5241989036167745074)
XLA Ops:
  7.2 0.0 copy-start
  7.2 0.0 all-gather.2.cloned.1.call-start
  7.2 0.7 all-gather.2.cloned.1.call-update
  7.9 0.0 reduce-scatter.3.cloned.1.call-start
  8.0 328.5 %all-gather.2.cloned.1.call-done = bf16[2048,1536]{0,1:T(8,128)(2,1)} async-done(((bf16[2048,24]{0,1:T(8,128)(2,1)}), bf16[2048,1536]{0,1:T(8,128)(2,1)}) %all-gather.2.cloned.1.call-update) | async-done | bytes 6291472 | tf_op jit(solution)/shard_map/all_gather | solution.py:17
  336.4 0.0 copy-done
  336.5 5.8 fusion
  342.2 0.0 copy-start.1
  342.2 0.0 copy-start.2
  342.2 0.0 reduce-scatter.3.cloned.1.call-update
  342.3 0.0 reduce-scatter.5.cloned.1.call-start
  342.3 102.7 %reduce-scatter.3.cloned.1.call-done = f32[256,192]{0,1:T(8,128)} async-done(((f32[256,1536]{0,1:T(8,128)}), f32[256,192]{0,1:T(8,128)}) %reduce-scatter.3.cloned.1.call-update) | async-done | bytes 196624 | tf_op jit(solution)/shard_map/reduce_scatter | solution.py:20
  445.0 0.9 convert_element_type.3
  446.0 25.4 %all_gather.7 = bf16[256,1536]{0,1:T(8,128)(2,1)S(1)} all-gather(bf16[256,192]{0,1:T(8,128)(2,1)S(1)} %convert_element_type.3), channel_id=1, replica_groups=mesh['aux'=8,'pair'=64] {'aux'}, dimensions={1}, use_global_device_ids=true | all-gather | bytes 884736 | tf_op jit(solution)/shard_map/all_gather | solution.py:23
  471.4 1.5 fusion.1
  472.9 0.0 reduce-scatter.5.cloned.1.call-update
  472.9 0.0 copy-done.1
  472.9 0.0 copy-done.2
  473.0 0.1 broadcast_subtract_fusion
  473.0 0.1 dynamic_slice.7
  473.1 0.1 dynamic_slice.6
  473.2 321.9 %reduce-scatter.5.cloned.1.call-done = f32[24,192]{1,0:T(8,128)} async-done(((f32[1536,192]{1,0:T(8,128)}), f32[24,192]{1,0:T(8,128)}) %reduce-scatter.5.cloned.1.call-update) | async-done | bytes 18448 | tf_op jit(solution)/shard_map/reduce_scatter | solution.py:24
  795.1 2.0 multiply_reduce_fusion
  797.2 150.5 %psum.7 = f32[]{:T(128)} all-reduce(f32[]{:T(128)} %get-tuple-element.2), channel_id=1, replica_groups=mesh['aux'=8,'pair'=64] {'aux','pair'}, use_global_device_ids=true, to_apply=%region_3.0 | all-reduce | flops 1 | bytes 8 | tf_op jit(solution)/shard_map/psum | solution.py:38
  (1 shorter events, 0.0 us)
Async XLA Ops:
  7.2 329.3 %copy-start = (bf16[256,2048]{1,0:T(8,128)(2,1)S(1)}, bf16[256,2048]{1,0:T(8,128)(2,1)}, u32[]{:S(2)}) copy-start(bf16[256,2048]{1,0:T(8,128)(2,1)} %param.4) | copy-start | bytes 3145732
  7.2 329.3 %all-gather.2.cloned.1.call-start = ((), (), s32[]{:S(2)}) async-start(), calls=%async_computation.2 | async-start | bytes 6389760 | tf_op jit(solution)/shard_map/all_gather | solution.py:17
  7.9 437.1 %reduce-scatter.3.cloned.1.call-start = ((), (), s32[]{:S(2)}) async-start(), calls=%async_computation.3 | async-start | bytes 1769472 | tf_op jit(solution)/shard_map/reduce_scatter | solution.py:20
  342.2 130.7 %copy-start.1 = (f32[768]{0:T(1024)S(1)}, f32[768]{0:T(1024)}, u32[]{:S(2)}) copy-start(f32[768]{0:T(1024)} %param.7) | copy-start | bytes 9220
  342.2 130.7 %copy-start.2 = (f32[2]{0:T(128)S(1)}, f32[2]{0:T(128)}, u32[]{:S(2)}) copy-start(f32[2]{0:T(128)} %param.6) | copy-start | bytes 28
  342.3 452.9 %reduce-scatter.5.cloned.1.call-start = ((), (), s32[]{:S(2)}) async-start(), calls=%async_computation.4 | async-start | bytes 1597440 | tf_op jit(solution)/shard_map/reduce_scatter | solution.py:24
Sparse Core Ops, SparseCore 0:
  10.1 326.3 all-gather.1
  342.4 102.6 reduce-scatter.2
  473.0 322.0 reduce-scatter.4
where the time goes:
time: 956 us
  waiting for transfers between devices  754 us (79%)
  blocking collectives  176 us (18%)
  between operations  15.6 us (2%)
    all_gather x1, waiting for transfers between devices, shards(): lax.all_gather(three_centre, 'pair', axis=1, tiled=True)  328 us
    reduce_scatter x1, waiting for transfers between devices, shards(): lax.psum_scatter(lax.dot_general(fitted, own_share, (((0,), (0,)), ((), (...  322 us
    psum x1, blocking collectives, shards(): energy = -lax.psum(local_energy, ('aux', 'pair'))  151 us
    reduce_scatter x1, waiting for transfers between devices, shards(): lax.psum_scatter(partial_fit, 'aux', scatter_dimension=1, tiled=True)  103 us
    all_gather x1, blocking collectives, shards(): fitted = lax.all_gather(own_share, 'aux', axis=1, tiled=True)  25.4 us
  transfers between devices with their start and end apart: 3, of which 3 were waited for; matrix products, arithmetic and copies ran while one was open for 0% of the time, Pallas kernels for 0%

commit v1 on v0

v1 whole, which is shorter than its diff:
```python
import functools

import jax
import jax.numpy as jnp
from jax import lax
from jax.experimental import pallas as pl
from jax.experimental.pallas import tpu as pltpu
from jax.sharding import PartitionSpec as P

MESH = pl.DeviceIdType.MESH
BF = jnp.bfloat16
F32 = jnp.float32
NT = (((1,), (1,)), ((), ()))


def kernel(
    l_ref, b_ref, occ_ref, virt_ref, amp_ref, en_ref,
    bt, fp, fx, zs, zr, fo, ft, ic, ra, rb, ia2, ib2, ra2, rb2, iz, rz, ih, rh, eb,
    zss, zrs, ags, agr, cs, cr, hs, hr, xs, xr, rss, rsr, z2s, z2r, h2s, h2r, es, er,
):
    aux = lax.axis_index("aux")
    pid = lax.axis_index("pair")
    c = aux % 2
    zh = aux // 2
    x = pid % 4
    y = (pid // 4) % 4
    zl = pid // 16

    def at_x(v):
        return (aux, zl * 16 + y * 4 + v)

    def at_y(v):
        return (aux, zl * 16 + v * 4 + x)

    def at_z(v):
        return (aux, v * 16 + y * 4 + x)

    def at_aux(v):
        return (v, pid)

    other = at_aux(zh * 2 + 1 - c)

    def remote(src, dst, ss, rs, dev):
        return pltpu.make_async_remote_copy(
            src_ref=src, dst_ref=dst, send_sem=ss, recv_sem=rs, device_id=dev, device_id_type=MESH
        )

    eye = (
        lax.broadcasted_iota(jnp.int32, (24, 24), 0) == lax.broadcasted_iota(jnp.int32, (24, 24), 1)
    ).astype(BF)
    bt[zl, y, x] = lax.dot_general(eye, b_ref[...], NT, preferred_element_type=F32).astype(BF)

    fo[...] = jnp.zeros_like(fo)
    barrier = pltpu.get_barrier_semaphore()
    for d in range(1, 4):
        for dev in (at_x((x + d) % 4), at_y((y + d) % 4), at_z((zl + d) % 4)):
            pl.semaphore_signal(barrier, inc=1, device_id=dev, device_id_type=MESH)
    for d in range(1, 8):
        pl.semaphore_signal(barrier, inc=1, device_id=at_aux((aux + d) % 8), device_id_type=MESH)
    pl.semaphore_wait(barrier, 16)

    sends = []

    def go(copy):
        copy.start()
        sends.append(copy)
        return copy

    zc = []
    for d in range(1, 4):
        zc.append(go(remote(bt.at[zl, y, x], bt.at[zl, y, x], zss.at[d - 1], zrs.at[d - 1], at_z((zl + d) % 4))))
    for d in range(1, 4):
        zc[d - 1].wait_recv()

    def gather_ring(blk, i0, at, n):
        right, left, opp = (i0 + 1) % 4, (i0 + 3) % 4, (i0 + 2) % 4

        def copy(i, h, j, to):
            return remote(blk(i, h), blk(i, h), ags.at[6 * n + j], agr.at[6 * n + j], at(to))

        def start():
            go(copy(i0, 0, 0, right))
            go(copy(i0, 1, 1, left))
            go(copy(i0, 1, 2, right))
            go(copy(i0, 0, 3, left))

        def forward():
            copy(left, 0, 0, right).wait_recv()
            go(copy(left, 0, 4, right))
            copy(right, 1, 1, left).wait_recv()
            go(copy(right, 1, 5, left))

        def finish():
            copy(left, 1, 2, right).wait_recv()
            copy(right, 0, 3, left).wait_recv()
            copy(opp, 0, 4, right).wait_recv()
            copy(opp, 1, 5, left).wait_recv()

        return start, forward, finish

    ka = pl.ds(0, 1024)
    kb = pl.ds(1024, 1024)
    halves = (pl.ds(0, 2), pl.ds(2, 2))

    def both(first, second):
        for a, b in zip(first, second):
            a()
            b()

    both(
        gather_ring(lambda i, h: bt.at[halves[h], i, x, :, ka], y, at_y, 0),
        gather_ring(lambda i, h: bt.at[halves[h], y, i, :, kb], x, at_x, 1),
    )
    both(
        gather_ring(lambda i, h: bt.at[halves[h], :, i, :, ka], x, at_x, 2),
        gather_ring(lambda i, h: bt.at[halves[h], i, :, :, kb], y, at_y, 3),
    )

    for z in range(4):
        for t in range(2):
            blk = bt[z, 2 * t : 2 * t + 2].reshape(192, 2048)
            n0 = (z * 2 + t) * 192
            res = lax.dot_general(l_ref[...], blk, NT, preferred_element_type=F32)
            fp[:, :, :, n0 : n0 + 192] = res.reshape(4, 2, 32, 192)

    cc = go(remote(fp.at[:, 1 - c], fx, cs.at[0], cr.at[0], other))
    cc.wait_recv()
    for q in range(4):
        fx[q] = fx[q] + fp[q, c]
        zs[q] = fx[q].astype(BF)

    def home(q):
        g2 = (0, 1, 2, 1)[q]
        return jnp.where(zl == 3, q, jnp.where(zl == 2, g2, jnp.where(zl == 1, q // 2, 0)))

    for q in range(4):
        hq = home(q)

        @pl.when((zh <= zl) & (hq != zh))
        def _():
            remote(zs.at[q], zr.at[q, zh], hs.at[q], hr.at[q, zh], at_aux(hq * 2 + c)).start()

    for q in range(4):
        hq = home(q)

        @pl.when(hq == zh)
        def _():
            for m in range(4):
                @pl.when((m <= zl) & (m != zh))
                def _():
                    remote(zs.at[q], zr.at[q, m], hs.at[q], hr.at[q, m], other).wait_recv()
                    fx[q] = fx[q] + zr[q, m].astype(F32)

            fo[q, c] = fx[q].astype(BF)
            remote(fo.at[q, c], fo.at[q, c], xs.at[q], xr.at[q], other).start()

    for q in range(4):
        @pl.when(home(q) == zh)
        def _():
            remote(fo.at[q, 1 - c], fo.at[q, 1 - c], xs.at[q], xr.at[q], other).wait_recv()

    ft[...] = fo[...].reshape(256, 1536).T
    rhs = jnp.concatenate([ft[pl.ds(pl.multiple_of((2 * j + c) * 192, 64), 192), :] for j in range(4)], axis=0)
    for z in range(4):
        for t in range(2):
            n0 = (z * 2 + t) * 192
            res = lax.dot_general(ft[n0 : n0 + 192, :], rhs, NT, preferred_element_type=F32)
            ic[z, 2 * t : 2 * t + 2] = res.astype(BF).reshape(2, 4, 24, 768)

    def reduce_ring(blk, rec, i0, at, n, out):
        right, left, opp = (i0 + 1) % 4, (i0 + 3) % 4, (i0 + 2) % 4

        def copy(i, h, j, to):
            return remote(blk(i, h), rec.at[j], rss.at[6 * n + j], rsr.at[6 * n + j], at(to))

        def start():
            go(copy(opp, 0, 0, right))
            go(copy(opp, 1, 1, left))
            go(copy(right, 1, 2, right))
            go(copy(left, 0, 3, left))

        def forward():
            copy(opp, 0, 0, right).wait_recv()
            b = blk(right, 0)
            b[...] = (b[...].astype(F32) + rec[0].astype(F32)).astype(BF)
            go(copy(right, 0, 4, right))
            copy(opp, 1, 1, left).wait_recv()
            b = blk(left, 1)
            b[...] = (b[...].astype(F32) + rec[1].astype(F32)).astype(BF)
            go(copy(left, 1, 5, left))

        def finish():
            for j in range(2, 6):
                copy(opp, 0, j, right).wait_recv()
            out(0, blk(i0, 0)[...].astype(F32) + rec[4].astype(F32) + rec[3].astype(F32))
            out(1, blk(i0, 1)[...].astype(F32) + rec[2].astype(F32) + rec[5].astype(F32))

        return start, forward, finish

    na = pl.ds(0, 384)
    nb = pl.ds(384, 384)

    def out_a(h, v):
        ia2[halves[h]] = v.astype(BF)

    def out_b(h, v):
        ib2[halves[h]] = v.astype(BF)

    both(
        reduce_ring(lambda i, h: ic.at[halves[h], :, i, :, na], ra, x, at_x, 0, out_a),
        reduce_ring(lambda i, h: ic.at[halves[h], i, :, :, nb], rb, y, at_y, 1, out_b),
    )

    def out_a2(h, v):
        iz[halves[h], :, na] = v

    def out_b2(h, v):
        iz[halves[h], :, nb] = v

    both(
        reduce_ring(lambda i, h: ia2.at[halves[h], i], ra2, y, at_y, 2, out_a2),
        reduce_ring(lambda i, h: ib2.at[halves[h], i], rb2, x, at_x, 3, out_b2),
    )
    z2 = []
    for d in range(1, 4):
        v = (zl + d) % 4
        z2.append(go(remote(iz.at[v], rz.at[d - 1], z2s.at[d - 1], z2r.at[d - 1], at_z(v))))
    for d in range(1, 4):
        z2[d - 1].wait_recv()
    tot = (iz[zl] + rz[0]) + (rz[1] + rz[2])
    for j in range(4):
        ih[j] = tot[:, 192 * j : 192 * j + 192]
    h2 = []
    for d in range(1, 4):
        v = (zh + d) % 4
        h2.append(go(remote(ih.at[v], rh.at[d - 1], h2s.at[d - 1], h2r.at[d - 1], at_aux(v * 2 + c))))
    for d in range(1, 4):
        h2[d - 1].wait_recv()
    integrals = (ih[zh] + rh[0]) + (rh[1] + rh[2])

    occ0, occ1 = occ_ref[0], occ_ref[1]
    virt = virt_ref[...]
    row = (pid % 32) * 24 + lax.broadcasted_iota(jnp.int32, (24, 768), 0)
    hit = row == lax.broadcasted_iota(jnp.int32, (24, 768), 1)
    row_gap = jnp.sum(jnp.where(hit, virt, 0.0), axis=1, keepdims=True) - jnp.where(pid >= 32, occ1, occ0)
    ca = aux % 4
    cols = [virt[:, 192 * j : 192 * j + 192] for j in range(4)]
    col = jnp.where(ca == 0, cols[0], jnp.where(ca == 1, cols[1], jnp.where(ca == 2, cols[2], cols[3])))
    col_gap = col - jnp.where(aux >= 4, occ1, occ0)
    amp = integrals / (row_gap + col_gap)
    amp_ref[...] = amp

    total = jnp.full((8, 128), jnp.sum(integrals * amp), F32)
    k = 0
    for place, size, at in ((x, 4, at_x), (y, 4, at_y), (zl, 4, at_z), (aux, 8, at_aux)):
        base = 8 * k
        eb[base + place] = total
        ecs = []
        for d in range(1, size):
            ecs.append(
                go(
                    remote(
                        eb.at[base + place], eb.at[base + place], es.at[base + d], er.at[base + d], at((place + d) % size)
                    )
                )
            )
        for e in ecs:
            e.wait_recv()
        total = eb[base]
        for i in range(1, size):
            total = total + eb[base + i]
        k += 1
    en_ref[...] = -total

    for s in sends:
        s.wait_send()
    for q in range(4):
        hq = home(q)

        @pl.when((zh <= zl) & (hq != zh))
        def _():
            remote(zs.at[q], zr.at[q, zh], hs.at[q], hr.at[q, zh], at_aux(hq * 2 + c)).wait_send()

        @pl.when(hq == zh)
        def _():
            remote(fo.at[q, c], fo.at[q, c], xs.at[q], xr.at[q], other).wait_send()


def shards(metric_factor, three_centre, occ_energy, virt_energy):
    vmem = pl.BlockSpec(memory_space=pltpu.VMEM)
    dma = pltpu.SemaphoreType.DMA
    amp, en = pl.pallas_call(
        kernel,
        out_shape=(jax.ShapeDtypeStruct((24, 192), F32), jax.ShapeDtypeStruct((8, 128), F32)),
        in_specs=[vmem, vmem, pl.BlockSpec(memory_space=pltpu.SMEM), vmem],
        out_specs=(vmem, vmem),
        scratch_shapes=[
            pltpu.VMEM((4, 4, 4, 24, 2048), BF),
            pltpu.VMEM((4, 2, 32, 1536), F32),
            pltpu.VMEM((4, 32, 1536), F32),
            pltpu.VMEM((4, 32, 1536), BF),
            pltpu.VMEM((4, 4, 32, 1536), BF),
            pltpu.VMEM((4, 2, 32, 1536), BF),
            pltpu.VMEM((1536, 256), BF),
            pltpu.VMEM((4, 4, 4, 24, 768), BF),
            pltpu.VMEM((6, 2, 4, 24, 384), BF),
            pltpu.VMEM((6, 2, 4, 24, 384), BF),
            pltpu.VMEM((4, 4, 24, 384), BF),
            pltpu.VMEM((4, 4, 24, 384), BF),
            pltpu.VMEM((6, 2, 24, 384), BF),
            pltpu.VMEM((6, 2, 24, 384), BF),
            pltpu.VMEM((4, 24, 768), F32),
            pltpu.VMEM((3, 24, 768), F32),
            pltpu.VMEM((4, 24, 192), F32),
            pltpu.VMEM((3, 24, 192), F32),
            pltpu.VMEM((32, 8, 128), F32),
            dma((3,)), dma((3,)),
            dma((24,)), dma((24,)),
            dma((1,)), dma((1,)),
            dma((4,)), dma((4, 4)),
            dma((4,)), dma((4,)),
            dma((24,)), dma((24,)),
            dma((3,)), dma((3,)),
            dma((3,)), dma((3,)),
            dma((32,)), dma((32,)),
        ],
        compiler_params=pltpu.CompilerParams(
            collective_id=0, has_side_effects=True, vmem_limit_bytes=56 * 1024 * 1024
        ),
    )(metric_factor, three_centre, occ_energy, virt_energy.reshape(1, -1))
    return amp, en[0, 0]


def solution(mesh):
    in_specs = (P("pair", "aux"), P("aux", "pair"), P(), P())
    out_specs = (P("pair", "aux"), P())
    return jax.shard_map(shards, mesh=mesh, in_specs=in_specs, out_specs=out_specs, check_vma=False)
```

time: 956 us -> 145 us (0.15)
  waiting for transfers between devices: 754 us -> 0 us
  blocking collectives: 176 us -> 0 us
  Pallas kernels: 0 us -> 139 us
  between operations: 15.6 us -> 0.64 us
    reduce_scatter x2 -> x0, waiting for transfers between devices: 425 us -> none  [the longest x1 322 us: shards(): lax.psum_scatter(lax.dot_general(fitted, own_share, (((0,), (0,)), ((), (...]
    all_gather x1 -> x0, waiting for transfers between devices: 328 us -> none  [shards(): lax.all_gather(three_centre, 'pair', axis=1, tiled=True)]
    psum x1 -> x0, blocking collectives: 151 us -> none  [shards(): energy = -lax.psum(local_energy, ('aux', 'pair'))]
    pallas_call x0 -> x1, Pallas kernels: none -> 139 us  [shards(): pl.pallas_call(kernel, out_shape=(jax.ShapeDtypeStruct((24, 192), F32), j...]
    all_gather x1 -> x0, blocking collectives: 25.4 us -> none  [shards(): fitted = lax.all_gather(own_share, 'aux', axis=1, tiled=True)]
  transfers between devices with their start and end apart: 3 -> 0, of which waited for: 3 -> 0; matrix products, arithmetic and copies ran while one was open for 0% -> 0% of each run, Pallas kernels for 0% -> 0%
where the time goes in v1:
time: 145 us
  Pallas kernels  139 us (96%)
  local copies, waits for them, and re-layouts  5.68 us (4%)
    pallas_call x1, Pallas kernels, shards(): pl.pallas_call(kernel, out_shape=(jax.ShapeDtypeStruct((24, 192), F32), j...  139 us
    unnamed x2, local copies, waits for them, and re-layouts  3.23 us

profile of v1, /device:TPU:1, one launch (start us, length us, event | category | flops | bytes accessed | tf_op | source)
XLA Modules:
  0.0 145.0 jit_solution(11452830461129183963)
XLA Ops:
  0.6 1.3 reshape.7.virt_ref
  1.9 1.9 %copy.6.b_ref = bf16[2048,24]{1,0:T(8,128)(2,1)} copy(bf16[2048,24]{0,1:T(8,128)(2,1)} %param.5) | data formatting | bytes 196608 | tf_op args[1]
  3.8 138.7 %shard_map.59 = (f32[24,192]{1,0:T(8,128)}, f32[8,128]{1,0:T(8,128)}) custom-call(bf16[256,2048]{1,0:T(8,128)(2,1)} %l_ref.1, bf16[2048,24]{1,0:T(8,128)(2,1)} %copy.6.b_ref, f32[2]{0:T(128)} %occ_ref.1, f32[1,768]{1,0:T(1,128)} %reshape.7.virt_ref), custom_call_target="tpu_custom_call" | custom-call | tf_op jit(solution)/shard_map/pallas_call | solution.py:292
  142.5 1.2 slice.3
  143.6 1.3 copy.8

commit v2 on v1

v2 whole, which is shorter than its diff:
```python
import jax
import jax.numpy as jnp
from jax import lax
from jax.experimental import pallas as pl
from jax.experimental.pallas import tpu as pltpu
from jax.sharding import PartitionSpec as P

MESH = pl.DeviceIdType.MESH
BF = jnp.bfloat16
F32 = jnp.float32
NT = (((1,), (1,)), ((), ()))


def kernel(
    l_hbm, b_hbm, occ_ref, virt_ref, amp_ref, en_ref,
    lv, bt, fp, fx, zs, zr, fo, ftn, ica, icb, ra, rb, ia2, ib2, ra2, rb2, iz, rz, ih, rh, ex, ez, ec,
    lsem, bsem, zss, zrs, ags, agr, cs, cr, hs, hr, xs, xr, rss, rsr, p2s, p2r, z2s, z2r, h2s, h2r,
    exs, exr, ezs, ezr, ecs, ecr,
):
    aux = lax.axis_index("aux")
    pid = lax.axis_index("pair")
    c = aux % 2
    zh = aux // 2
    x = pid % 4
    y = (pid // 4) % 4
    zl = pid // 16

    def at_x(v):
        return (aux, zl * 16 + y * 4 + v)

    def at_y(v):
        return (aux, zl * 16 + v * 4 + x)

    def at_z(v):
        return (aux, v * 16 + y * 4 + x)

    def at_aux(v):
        return (v, pid)

    def at_plane(d):
        return (aux, zl * 16 + ((y + d // 4) % 4) * 4 + (x + d % 4) % 4)

    def at_column(d):
        v = (zh * 4 + zl + d) % 16
        return ((v // 4) * 2 + c, (v % 4) * 16 + y * 4 + x)

    other = at_aux(zh * 2 + 1 - c)

    def remote(src, dst, ss, rs, dev):
        return pltpu.make_async_remote_copy(
            src_ref=src, dst_ref=dst, send_sem=ss, recv_sem=rs, device_id=dev, device_id_type=MESH
        )

    def home(q):
        return jnp.where(zl == 3, q, jnp.where(zl == 2, (0, 1, 2, 1)[q], jnp.where(zl == 1, q // 2, 0)))

    def to_home(j, q, m, dev):
        return remote(zs.at[j, q], zr.at[j, q, m], hs.at[j, q], hr.at[j, q, m], dev)

    def to_other(j, q):
        return remote(fo.at[j, q, c], fo.at[j, q, c], xs.at[j, q], xr.at[j, q], other)

    sends = []

    def go(copy):
        copy.start()
        sends.append(copy)
        return copy

    def drain(k):
        for s in sends:
            s.wait_send()
        if k < 5:
            return
        for q in range(4):
            hq = home(q)

            @pl.when((zh <= zl) & (hq != zh))
            def _():
                for j in range(3):
                    to_home(j, q, zh, at_aux(hq * 2 + c)).wait_send()

            @pl.when(hq == zh)
            def _():
                for j in range(3):
                    to_other(j, q).wait_send()

    barrier = pltpu.get_barrier_semaphore()
    for d in range(1, 16):
        pl.semaphore_signal(barrier, inc=1, device_id=at_plane(d), device_id_type=MESH)
        pl.semaphore_signal(barrier, inc=1, device_id=at_column(d), device_id_type=MESH)
    pl.semaphore_signal(barrier, inc=1, device_id=other, device_id_type=MESH)
    own = []
    for j in range(3):
        b = pltpu.make_async_copy(b_hbm.at[pl.ds(8 * j, 8)], bt.at[j, zl, y, x], bsem.at[j])
        b.start()
        own.append(b)
    lcopy = pltpu.make_async_copy(l_hbm, lv, lsem.at[0])
    lcopy.start()
    fo[...] = jnp.zeros_like(fo)
    for b in own:
        b.wait()
    pl.semaphore_wait(barrier, 31)

    def z_copy(j, d):
        return remote(
            bt.at[j, zl, y, x], bt.at[j, zl, y, x], zss.at[3 * j + d - 1], zrs.at[3 * j + d - 1], at_z((zl + d) % 4)
        )

    def z_wait(j):
        for d in range(1, 4):
            z_copy(j, d).wait_recv()

    for j in range(3):
        for d in range(1, 4):
            go(z_copy(j, d))

    def gather_ring(blk, i0, at, n):
        right, left, opp = (i0 + 1) % 4, (i0 + 3) % 4, (i0 + 2) % 4

        def copy(i, h, k, to):
            return remote(blk(i, h), blk(i, h), ags.at[6 * n + k], agr.at[6 * n + k], at(to))

        def start():
            go(copy(i0, 0, 0, right))
            go(copy(i0, 1, 1, left))
            go(copy(i0, 1, 2, right))
            go(copy(i0, 0, 3, left))

        def forward():
            copy(left, 0, 0, right).wait_recv()
            go(copy(left, 0, 4, right))
            copy(right, 1, 1, left).wait_recv()
            go(copy(right, 1, 5, left))

        def finish():
            copy(left, 1, 2, right).wait_recv()
            copy(right, 0, 3, left).wait_recv()
            copy(opp, 0, 4, right).wait_recv()
            copy(opp, 1, 5, left).wait_recv()

        return start, forward, finish

    ka = pl.ds(0, 1024)
    kb = pl.ds(1024, 1024)
    halves = (pl.ds(0, 2), pl.ds(2, 2))

    def second(j):
        a = gather_ring(lambda i, h: bt.at[j, halves[h], i, x, :, ka], y, at_y, 4 * j)
        b = gather_ring(lambda i, h: bt.at[j, halves[h], y, i, :, kb], x, at_x, 4 * j + 1)
        return a, b

    def third(j):
        a = gather_ring(lambda i, h: bt.at[j, halves[h], :, i, :, ka], x, at_x, 4 * j + 2)
        b = gather_ring(lambda i, h: bt.at[j, halves[h], i, :, :, kb], y, at_y, 4 * j + 3)
        return a, b

    r2 = [second(j) for j in range(3)]
    r3 = [third(j) for j in range(3)]

    def run(rings, step):
        for r in rings:
            r[step]()

    def core_copy(j):
        return remote(fp.at[j, :, 1 - c], fx.at[j], cs.at[j], cr.at[j], other)

    def fit(j):
        for t in range(2):
            blk = bt[j, 2 * t : 2 * t + 2].reshape(256, 2048)
            res = lax.dot_general(lv[...], blk, NT, preferred_element_type=F32)
            fp[j, :, :, :, 256 * t : 256 * t + 256] = res.reshape(4, 2, 32, 256)
        go(core_copy(j))

    def send_home(j):
        core_copy(j).wait_recv()
        for q in range(4):
            fx[j, q] = fx[j, q] + fp[j, q, c]
            zs[j, q] = fx[j, q].astype(BF)
            hq = home(q)

            @pl.when((zh <= zl) & (hq != zh))
            def _():
                to_home(j, q, zh, at_aux(hq * 2 + c)).start()

    def finish_home(j):
        for q in range(4):
            @pl.when(home(q) == zh)
            def _():
                for m in range(4):
                    @pl.when((m <= zl) & (m != zh))
                    def _():
                        to_home(j, q, m, other).wait_recv()
                        fx[j, q] = fx[j, q] + zr[j, q, m].astype(F32)

                fo[j, q, c] = fx[j, q].astype(BF)
                to_other(j, q).start()

    def finish_rows(j):
        for q in range(4):
            @pl.when(home(q) == zh)
            def _():
                remote(fo.at[j, q, 1 - c], fo.at[j, q, 1 - c], xs.at[j, q], xr.at[j, q], other).wait_recv()

        ftn[:, j] = fo[j].reshape(256, 512).T.reshape(64, 8, 256)

    z_wait(0)
    run(r2[0], 0)
    z_wait(1)
    run(r2[1], 0)
    run(r2[0], 1)
    z_wait(2)
    run(r2[2], 0)
    run(r2[0], 2)
    run(r3[0], 0)
    run(r2[1], 1)
    run(r2[2], 1)
    run(r2[1], 2)
    run(r3[0], 1)
    run(r3[1], 0)
    run(r2[2], 2)
    lcopy.wait()
    run(r3[0], 2)
    fit(0)
    run(r3[1], 1)
    run(r3[2], 0)
    send_home(0)
    run(r3[1], 2)
    fit(1)
    run(r3[2], 1)
    send_home(1)
    finish_home(0)
    run(r3[2], 2)
    fit(2)
    finish_rows(0)
    send_home(2)
    finish_home(1)
    finish_rows(1)
    finish_home(2)
    finish_rows(2)

    def integrals_of(half, ic):
        rhs = jnp.concatenate(
            [ftn[pl.ds((4 * half + 2 * t + c) * 8, 8)].reshape(192, 256) for t in range(2)], axis=0
        )
        for z in range(4):
            lhs = ftn[16 * z : 16 * z + 16].reshape(384, 256)
            res = lax.dot_general(lhs, rhs, NT, preferred_element_type=F32)
            ic[z] = res.astype(BF).reshape(4, 4, 24, 384)

    def reduce_ring(blk, rec, i0, at, n, out):
        right, left, opp = (i0 + 1) % 4, (i0 + 3) % 4, (i0 + 2) % 4

        def copy(i, h, k, to):
            return remote(blk(i, h), rec.at[k], rss.at[6 * n + k], rsr.at[6 * n + k], at(to))

        def start():
            go(copy(opp, 0, 0, right))
            go(copy(opp, 1, 1, left))
            go(copy(right, 1, 2, right))
            go(copy(left, 0, 3, left))

        def forward():
            copy(opp, 0, 0, right).wait_recv()
            b = blk(right, 0)
            b[...] = (b[...].astype(F32) + rec[0].astype(F32)).astype(BF)
            go(copy(right, 0, 4, right))
            copy(opp, 1, 1, left).wait_recv()
            b = blk(left, 1)
            b[...] = (b[...].astype(F32) + rec[1].astype(F32)).astype(BF)
            go(copy(left, 1, 5, left))

        def finish():
            for k in range(2, 6):
                copy(opp, 0, k, right).wait_recv()
            out(0, blk(i0, 0)[...].astype(F32) + rec[4].astype(F32) + rec[3].astype(F32))
            out(1, blk(i0, 1)[...].astype(F32) + rec[2].astype(F32) + rec[5].astype(F32))

        return start, forward, finish

    def out_a(h, v):
        ia2[halves[h]] = v.astype(BF)

    def out_b(h, v):
        ib2[halves[h]] = v.astype(BF)

    ring_a = reduce_ring(lambda i, h: ica.at[halves[h], :, i], ra, x, at_x, 0, out_a)
    ring_b = reduce_ring(lambda i, h: icb.at[halves[h], i], rb, y, at_y, 1, out_b)
    integrals_of(0, ica)
    ring_a[0]()
    integrals_of(1, icb)
    ring_b[0]()
    ring_a[1]()
    ring_b[1]()
    ring_a[2]()

    def direct_a(d):
        v = (y + d) % 4
        return remote(ia2.at[:, v], ra2.at[d - 1], p2s.at[d - 1], p2r.at[d - 1], at_y(v))

    def direct_b(d):
        v = (x + d) % 4
        return remote(ib2.at[:, v], rb2.at[d - 1], p2s.at[d + 2], p2r.at[d + 2], at_x(v))

    for d in (2, 1, 3):
        go(direct_a(d))
    ring_b[2]()
    for d in (2, 1, 3):
        go(direct_b(d))
    for d in (1, 3, 2):
        direct_a(d).wait_recv()
    mine = ia2[:, y].astype(F32) + ra2[0].astype(F32) + ra2[1].astype(F32) + ra2[2].astype(F32)
    iz[:, :, 0:384] = mine
    for d in (1, 3, 2):
        direct_b(d).wait_recv()
    mine = ib2[:, x].astype(F32) + rb2[0].astype(F32) + rb2[1].astype(F32) + rb2[2].astype(F32)
    iz[:, :, 384:768] = mine
    z2 = []
    for d in range(1, 4):
        v = (zl + d) % 4
        z2.append(go(remote(iz.at[v], rz.at[d - 1], z2s.at[d - 1], z2r.at[d - 1], at_z(v))))
    for d in range(1, 4):
        z2[d - 1].wait_recv()
    tot = (iz[zl] + rz[0]) + (rz[1] + rz[2])
    for t in range(4):
        ih[t] = tot[:, 192 * t : 192 * t + 192]
    h2 = []
    for d in range(1, 4):
        v = (zh + d) % 4
        h2.append(go(remote(ih.at[v], rh.at[d - 1], h2s.at[d - 1], h2r.at[d - 1], at_aux(v * 2 + c))))
    for d in range(1, 4):
        h2[d - 1].wait_recv()
    integrals = (ih[zh] + rh[0]) + (rh[1] + rh[2])

    occ0, occ1 = occ_ref[0], occ_ref[1]
    virt = virt_ref[...].reshape(1, 768)
    row = (pid % 32) * 24 + lax.broadcasted_iota(jnp.int32, (24, 768), 0)
    hit = row == lax.broadcasted_iota(jnp.int32, (24, 768), 1)
    row_gap = jnp.sum(jnp.where(hit, virt, 0.0), axis=1, keepdims=True) - jnp.where(pid >= 32, occ1, occ0)
    ca = aux % 4
    cols = [virt[:, 192 * t : 192 * t + 192] for t in range(4)]
    col = jnp.where(ca == 0, cols[0], jnp.where(ca == 1, cols[1], jnp.where(ca == 2, cols[2], cols[3])))
    col_gap = col - jnp.where(aux >= 4, occ1, occ0)
    amp = integrals / (row_gap + col_gap)
    amp_ref[...] = amp

    total = jnp.full((8, 128), jnp.sum(integrals * amp), F32)
    for buf, place, size, at, ss, rs in (
        (ex, y * 4 + x, 16, at_plane, exs, exr),
        (ez, zh * 4 + zl, 16, at_column, ezs, ezr),
        (ec, c, 2, lambda d: other, ecs, ecr),
    ):
        buf[place] = total
        waits = [go(remote(buf.at[place], buf.at[place], ss.at[d], rs.at[d], at(d))) for d in range(1, size)]
        for w in waits:
            w.wait_recv()
        total = buf[0]
        for i in range(1, size):
            total = total + buf[i]
    en_ref[...] = -total[0:1, 0:1]
    drain(9)


def shards(metric_factor, three_centre, occ_energy, virt_energy):
    vmem = pl.BlockSpec(memory_space=pltpu.VMEM)
    hbm = pl.BlockSpec(memory_space=pl.ANY)
    dma = pltpu.SemaphoreType.DMA
    amp, en = pl.pallas_call(
        kernel,
        out_shape=(jax.ShapeDtypeStruct((24, 192), F32), jax.ShapeDtypeStruct((1, 1), F32)),
        in_specs=[hbm, hbm, pl.BlockSpec(memory_space=pltpu.SMEM), vmem],
        out_specs=(vmem, vmem),
        scratch_shapes=[
            pltpu.VMEM((256, 2048), BF),
            pltpu.VMEM((3, 4, 4, 4, 8, 2048), BF),
            pltpu.VMEM((3, 4, 2, 32, 512), F32),
            pltpu.VMEM((3, 4, 32, 512), F32),
            pltpu.VMEM((3, 4, 32, 512), BF),
            pltpu.VMEM((3, 4, 4, 32, 512), BF),
            pltpu.VMEM((3, 4, 2, 32, 512), BF),
            pltpu.VMEM((64, 3, 8, 256), BF),
            pltpu.VMEM((4, 4, 4, 24, 384), BF),
            pltpu.VMEM((4, 4, 4, 24, 384), BF),
            pltpu.VMEM((6, 2, 4, 24, 384), BF),
            pltpu.VMEM((6, 2, 4, 24, 384), BF),
            pltpu.VMEM((4, 4, 24, 384), BF),
            pltpu.VMEM((4, 4, 24, 384), BF),
            pltpu.VMEM((3, 4, 24, 384), BF),
            pltpu.VMEM((3, 4, 24, 384), BF),
            pltpu.VMEM((4, 24, 768), F32),
            pltpu.VMEM((3, 24, 768), F32),
            pltpu.VMEM((4, 24, 192), F32),
            pltpu.VMEM((3, 24, 192), F32),
            pltpu.VMEM((16, 8, 128), F32),
            pltpu.VMEM((16, 8, 128), F32),
            pltpu.VMEM((2, 8, 128), F32),
            dma((1,)), dma((3,)),
            dma((9,)), dma((9,)),
            dma((72,)), dma((72,)),
            dma((3,)), dma((3,)),
            dma((3, 4)), dma((3, 4, 4)),
            dma((3, 4)), dma((3, 4)),
            dma((12,)), dma((12,)),
            dma((6,)), dma((6,)),
            dma((3,)), dma((3,)),
            dma((3,)), dma((3,)),
            dma((16,)), dma((16,)),
            dma((16,)), dma((16,)),
            dma((2,)), dma((2,)),
        ],
        compiler_params=pltpu.CompilerParams(
            collective_id=0, has_side_effects=True, vmem_limit_bytes=56 * 1024 * 1024
        ),
    )(metric_factor, three_centre.T, occ_energy, virt_energy)
    return amp, en.reshape(())


def solution(mesh):
    in_specs = (P("pair", "aux"), P("aux", "pair"), P(), P())
    out_specs = (P("pair", "aux"), P())
    return jax.shard_map(shards, mesh=mesh, in_specs=in_specs, out_specs=out_specs, check_vma=False)
```

time: 145 us -> 130 us (0.90)
  Pallas kernels: 139 us -> 126 us
  local copies, waits for them, and re-layouts: 5.68 us -> 1.35 us
  between operations: 0.64 us -> 2.4 us
    pallas_call x1, Pallas kernels: 139 us -> 126 us  [shards(): pl.pallas_call(kernel, out_shape=(jax.ShapeDtypeStruct((24, 192), F32), j...]
    unnamed x2 -> x1, local copies, waits for them, and re-layouts: 3.23 us -> 1.35 us
where the time goes in v2:
time: 130 us
  Pallas kernels  126 us (97%)
  between operations  2.4 us (2%)
  local copies, waits for them, and re-layouts  1.35 us (1%)
    pallas_call x1, Pallas kernels, shards(): pl.pallas_call(kernel, out_shape=(jax.ShapeDtypeStruct((24, 192), F32), j...  126 us

profile of v2, /device:TPU:1, one launch (start us, length us, event | category | flops | bytes accessed | tf_op | source)
XLA Modules:
  0.0 129.5 jit_solution(16546754350498255357)
XLA Ops:
  0.6 125.8 %shard_map.59 = (f32[24,192]{1,0:T(8,128)}, f32[1,1]{1,0:T(1,128)}) custom-call(bf16[256,2048]{1,0:T(8,128)(2,1)} %l_hbm.1, bf16[24,2048]{1,0:T(8,128)(2,1)} %bitcast.2, f32[2]{0:T(128)} %occ_ref.1, f32[768]{0:T(1024)} %virt_ref.1), custom_call_target="tpu_custom_call" | custom-call | tf_op jit(solution)/shard_map/pallas_call | solution.py:368
  126.4 1.3 %copy.8 = f32[24,192]{1,0:T(8,128)} copy(f32[24,192]{1,0:T(8,128)} %get-tuple-element.8) | data formatting | bytes 36864

commit v3 on v2

--- a/solution.py
+++ b/solution.py
@@ -102,18 +102,43 @@
         b.wait()
     pl.semaphore_wait(barrier, 31)
 
-    def z_copy(j, d):
-        return remote(
-            bt.at[j, zl, y, x], bt.at[j, zl, y, x], zss.at[3 * j + d - 1], zrs.at[3 * j + d - 1], at_z((zl + d) % 4)
-        )
-
-    def z_wait(j):
-        for d in range(1, 4):
-            z_copy(j, d).wait_recv()
-
-    for j in range(3):
-        for d in range(1, 4):
-            go(z_copy(j, d))
+    ka = pl.ds(0, 1024)
+    kb = pl.ds(1024, 1024)
+    halves = (pl.ds(0, 2), pl.ds(2, 2))
+
+    def exchange(blk, i0, at, n):
+        def copy(d):
+            return remote(blk, blk, zss.at[3 * n + d - 1], zrs.at[3 * n + d - 1], at((i0 + d) % 4))
+
+        def start():
+            for d in (2, 1, 3):
+                go(copy(d))
+
+        def finish():
+            for d in (1, 3, 2):
+                copy(d).wait_recv()
+
+        return start, finish
+
+    z0 = exchange(bt.at[0, zl, y, x], zl, at_z, 0)
+    s0 = [
+        exchange(bt.at[0, :, y, x, :, ka], y, at_y, 1),
+        exchange(bt.at[0, :, y, x, :, kb], x, at_x, 2),
+    ]
+    f12 = [
+        [
+            exchange(bt.at[j, zl, y, x, :, ka], y, at_y, 4 * j - 1),
+            exchange(bt.at[j, zl, y, x, :, kb], x, at_x, 4 * j),
+        ]
+        for j in (1, 2)
+    ]
+    z12 = [
+        [
+            exchange(bt.at[j, zl, :, x, :, ka], zl, at_z, 4 * j + 1),
+            exchange(bt.at[j, zl, y, :, :, kb], zl, at_z, 4 * j + 2),
+        ]
+        for j in (1, 2)
+    ]
 
     def gather_ring(blk, i0, at, n):
         right, left, opp = (i0 + 1) % 4, (i0 + 3) % 4, (i0 + 2) % 4
@@ -141,21 +166,11 @@
 
         return start, forward, finish
 
-    ka = pl.ds(0, 1024)
-    kb = pl.ds(1024, 1024)
-    halves = (pl.ds(0, 2), pl.ds(2, 2))
-
-    def second(j):
-        a = gather_ring(lambda i, h: bt.at[j, halves[h], i, x, :, ka], y, at_y, 4 * j)
-        b = gather_ring(lambda i, h: bt.at[j, halves[h], y, i, :, kb], x, at_x, 4 * j + 1)
+    def third(j):
+        a = gather_ring(lambda i, h: bt.at[j, halves[h], :, i, :, ka], x, at_x, 2 * j)
+        b = gather_ring(lambda i, h: bt.at[j, halves[h], i, :, :, kb], y, at_y, 2 * j + 1)
         return a, b
 
-    def third(j):
-        a = gather_ring(lambda i, h: bt.at[j, halves[h], :, i, :, ka], x, at_x, 4 * j + 2)
-        b = gather_ring(lambda i, h: bt.at[j, halves[h], i, :, :, kb], y, at_y, 4 * j + 3)
-        return a, b
-
-    r2 = [second(j) for j in range(3)]
     r3 = [third(j) for j in range(3)]
 
     def run(rings, step):
@@ -204,36 +219,35 @@
 
         ftn[:, j] = fo[j].reshape(256, 512).T.reshape(64, 8, 256)
 
-    z_wait(0)
-    run(r2[0], 0)
-    z_wait(1)
-    run(r2[1], 0)
-    run(r2[0], 1)
-    z_wait(2)
-    run(r2[2], 0)
-    run(r2[0], 2)
+    z0[0]()
+    for f in f12:
+        run(f, 0)
+    z0[1]()
+    run(s0, 0)
+    for f, z in zip(f12, z12):
+        run(f, 1)
+        run(z, 0)
+    run(s0, 1)
     run(r3[0], 0)
-    run(r2[1], 1)
-    run(r2[2], 1)
-    run(r2[1], 2)
     run(r3[0], 1)
+    run(z12[0], 1)
     run(r3[1], 0)
-    run(r2[2], 2)
     lcopy.wait()
     run(r3[0], 2)
     fit(0)
+    send_home(0)
     run(r3[1], 1)
+    run(z12[1], 1)
     run(r3[2], 0)
-    send_home(0)
     run(r3[1], 2)
     fit(1)
+    send_home(1)
     run(r3[2], 1)
-    send_home(1)
-    finish_home(0)
     run(r3[2], 2)
     fit(2)
+    finish_home(0)
+    send_home(2)
     finish_rows(0)
-    send_home(2)
     finish_home(1)
     finish_rows(1)
     finish_home(2)
@@ -395,8 +409,8 @@
             pltpu.VMEM((16, 8, 128), F32),
             pltpu.VMEM((2, 8, 128), F32),
             dma((1,)), dma((3,)),
-            dma((9,)), dma((9,)),
-            dma((72,)), dma((72,)),
+            dma((33,)), dma((33,)),
+            dma((36,)), dma((36,)),
             dma((3,)), dma((3,)),
             dma((3, 4)), dma((3, 4, 4)),
             dma((3, 4)), dma((3, 4)),

time: 130 us -> 124 us (0.954)
  Pallas kernels: 126 us -> 120 us
    pallas_call x1, Pallas kernels: 126 us -> 120 us  [shards(): pl.pallas_call(kernel, out_shape=(jax.ShapeDtypeStruct((24, 192), F32), j...]
where the time goes in v3:
time: 124 us
  Pallas kernels  120 us (97%)
  between operations  2.4 us (2%)
  local copies, waits for them, and re-layouts  1.35 us (1%)
    pallas_call x1, Pallas kernels, shards(): pl.pallas_call(kernel, out_shape=(jax.ShapeDtypeStruct((24, 192), F32), j...  120 us

profile of v3, /device:TPU:1, one launch (start us, length us, event | category | flops | bytes accessed | tf_op | source)
XLA Modules:
  0.0 123.7 jit_solution(12502972582215494594)
XLA Ops:
  0.6 120.0 %shard_map.59 = (f32[24,192]{1,0:T(8,128)}, f32[1,1]{1,0:T(1,128)}) custom-call(bf16[256,2048]{1,0:T(8,128)(2,1)} %l_hbm.1, bf16[24,2048]{1,0:T(8,128)(2,1)} %bitcast.2, f32[2]{0:T(128)} %occ_ref.1, f32[768]{0:T(1024)} %virt_ref.1), custom_call_target="tpu_custom_call" | custom-call | tf_op jit(solution)/shard_map/pallas_call | solution.py:382
  120.6 1.3 %copy.8 = f32[24,192]{1,0:T(8,128)} copy(f32[24,192]{1,0:T(8,128)} %get-tuple-element.8) | data formatting | bytes 36864

commit v4 on v3

--- a/solution.py
+++ b/solution.py
@@ -9,11 +9,30 @@
 BF = jnp.bfloat16
 F32 = jnp.float32
 NT = (((1,), (1,)), ((), ()))
+ROWS = (16, 8)
+JS = (slice(0, 2), slice(2, 3))
+
+
+def part_buffers(r):
+    return [
+        pltpu.VMEM((4, 4, 4, r, 384), BF),
+        pltpu.VMEM((4, 4, 4, r, 384), BF),
+        pltpu.VMEM((6, 2, 4, r, 384), BF),
+        pltpu.VMEM((6, 2, 4, r, 384), BF),
+        pltpu.VMEM((4, 4, r, 384), BF),
+        pltpu.VMEM((4, 4, r, 384), BF),
+        pltpu.VMEM((3, 4, r, 384), BF),
+        pltpu.VMEM((3, 4, r, 384), BF),
+        pltpu.VMEM((4, r, 768), F32),
+        pltpu.VMEM((3, r, 768), F32),
+        pltpu.VMEM((4, r, 192), F32),
+        pltpu.VMEM((3, r, 192), F32),
+    ]
 
 
 def kernel(
     l_hbm, b_hbm, occ_ref, virt_ref, amp_ref, en_ref,
-    lv, bt, fp, fx, zs, zr, fo, ftn, ica, icb, ra, rb, ia2, ib2, ra2, rb2, iz, rz, ih, rh, ex, ez, ec,
+    lv, bt, fp, fx, zs, zr, fo, ftn, parts, ex, ez, ec,
     lsem, bsem, zss, zrs, ags, agr, cs, cr, hs, hr, xs, xr, rss, rsr, p2s, p2r, z2s, z2r, h2s, h2r,
     exs, exr, ezs, ezr, ecs, ecr,
 ):
@@ -120,25 +139,16 @@
 
         return start, finish
 
-    z0 = exchange(bt.at[0, zl, y, x], zl, at_z, 0)
-    s0 = [
-        exchange(bt.at[0, :, y, x, :, ka], y, at_y, 1),
-        exchange(bt.at[0, :, y, x, :, kb], x, at_x, 2),
+    z01 = [exchange(bt.at[j, zl, y, x], zl, at_z, j) for j in range(2)]
+    s01 = [
+        [
+            exchange(bt.at[j, :, y, x, :, ka], y, at_y, 2 * j + 2),
+            exchange(bt.at[j, :, y, x, :, kb], x, at_x, 2 * j + 3),
+        ]
+        for j in range(2)
     ]
-    f12 = [
-        [
-            exchange(bt.at[j, zl, y, x, :, ka], y, at_y, 4 * j - 1),
-            exchange(bt.at[j, zl, y, x, :, kb], x, at_x, 4 * j),
-        ]
-        for j in (1, 2)
-    ]
-    z12 = [
-        [
-            exchange(bt.at[j, zl, :, x, :, ka], zl, at_z, 4 * j + 1),
-            exchange(bt.at[j, zl, y, :, :, kb], zl, at_z, 4 * j + 2),
-        ]
-        for j in (1, 2)
-    ]
+    f2 = [exchange(bt.at[2, zl, y, x, :, ka], y, at_y, 6), exchange(bt.at[2, zl, y, x, :, kb], x, at_x, 7)]
+    z2 = [exchange(bt.at[2, zl, :, x, :, ka], zl, at_z, 8), exchange(bt.at[2, zl, y, :, :, kb], zl, at_z, 9)]
 
     def gather_ring(blk, i0, at, n):
         right, left, opp = (i0 + 1) % 4, (i0 + 3) % 4, (i0 + 2) % 4
@@ -219,25 +229,26 @@
 
         ftn[:, j] = fo[j].reshape(256, 512).T.reshape(64, 8, 256)
 
-    z0[0]()
-    for f in f12:
-        run(f, 0)
-    z0[1]()
-    run(s0, 0)
-    for f, z in zip(f12, z12):
-        run(f, 1)
-        run(z, 0)
-    run(s0, 1)
+    z01[0][0]()
+    z01[1][0]()
+    run(f2, 0)
+    z01[0][1]()
+    run(s01[0], 0)
+    z01[1][1]()
+    run(s01[1], 0)
+    run(s01[0], 1)
     run(r3[0], 0)
+    run(f2, 1)
+    run(z2, 0)
     run(r3[0], 1)
-    run(z12[0], 1)
+    run(s01[1], 1)
     run(r3[1], 0)
     lcopy.wait()
     run(r3[0], 2)
     fit(0)
     send_home(0)
     run(r3[1], 1)
-    run(z12[1], 1)
+    run(z2, 1)
     run(r3[2], 0)
     run(r3[1], 2)
     fit(1)
@@ -253,14 +264,16 @@
     finish_home(2)
     finish_rows(2)
 
-    def integrals_of(half, ic):
-        rhs = jnp.concatenate(
-            [ftn[pl.ds((4 * half + 2 * t + c) * 8, 8)].reshape(192, 256) for t in range(2)], axis=0
-        )
+    rhs = [
+        jnp.concatenate([ftn[pl.ds((4 * f + 2 * t + c) * 8, 8)].reshape(192, 256) for t in range(2)], axis=0)
+        for f in range(2)
+    ]
+
+    def integrals_of(k, f, ic):
         for z in range(4):
-            lhs = ftn[16 * z : 16 * z + 16].reshape(384, 256)
-            res = lax.dot_general(lhs, rhs, NT, preferred_element_type=F32)
-            ic[z] = res.astype(BF).reshape(4, 4, 24, 384)
+            lhs = ftn[16 * z : 16 * z + 16, JS[k]].reshape(16 * ROWS[k], 256)
+            res = lax.dot_general(lhs, rhs[f], NT, preferred_element_type=F32)
+            ic[z] = res.astype(BF).reshape(4, 4, ROWS[k], 384)
 
     def reduce_ring(blk, rec, i0, at, n, out):
         right, left, opp = (i0 + 1) % 4, (i0 + 3) % 4, (i0 + 2) % 4
@@ -292,59 +305,81 @@
 
         return start, forward, finish
 
-    def out_a(h, v):
-        ia2[halves[h]] = v.astype(BF)
-
-    def out_b(h, v):
-        ib2[halves[h]] = v.astype(BF)
-
-    ring_a = reduce_ring(lambda i, h: ica.at[halves[h], :, i], ra, x, at_x, 0, out_a)
-    ring_b = reduce_ring(lambda i, h: icb.at[halves[h], i], rb, y, at_y, 1, out_b)
-    integrals_of(0, ica)
-    ring_a[0]()
-    integrals_of(1, icb)
-    ring_b[0]()
-    ring_a[1]()
-    ring_b[1]()
-    ring_a[2]()
-
-    def direct_a(d):
-        v = (y + d) % 4
-        return remote(ia2.at[:, v], ra2.at[d - 1], p2s.at[d - 1], p2r.at[d - 1], at_y(v))
-
-    def direct_b(d):
-        v = (x + d) % 4
-        return remote(ib2.at[:, v], rb2.at[d - 1], p2s.at[d + 2], p2r.at[d + 2], at_x(v))
-
-    for d in (2, 1, 3):
-        go(direct_a(d))
-    ring_b[2]()
-    for d in (2, 1, 3):
-        go(direct_b(d))
-    for d in (1, 3, 2):
-        direct_a(d).wait_recv()
-    mine = ia2[:, y].astype(F32) + ra2[0].astype(F32) + ra2[1].astype(F32) + ra2[2].astype(F32)
-    iz[:, :, 0:384] = mine
-    for d in (1, 3, 2):
-        direct_b(d).wait_recv()
-    mine = ib2[:, x].astype(F32) + rb2[0].astype(F32) + rb2[1].astype(F32) + rb2[2].astype(F32)
-    iz[:, :, 384:768] = mine
-    z2 = []
-    for d in range(1, 4):
-        v = (zl + d) % 4
-        z2.append(go(remote(iz.at[v], rz.at[d - 1], z2s.at[d - 1], z2r.at[d - 1], at_z(v))))
-    for d in range(1, 4):
-        z2[d - 1].wait_recv()
-    tot = (iz[zl] + rz[0]) + (rz[1] + rz[2])
-    for t in range(4):
-        ih[t] = tot[:, 192 * t : 192 * t + 192]
-    h2 = []
-    for d in range(1, 4):
-        v = (zh + d) % 4
-        h2.append(go(remote(ih.at[v], rh.at[d - 1], h2s.at[d - 1], h2r.at[d - 1], at_aux(v * 2 + c))))
-    for d in range(1, 4):
-        h2[d - 1].wait_recv()
-    integrals = (ih[zh] + rh[0]) + (rh[1] + rh[2])
+    def store(dst):
+        def out(h, v):
+            dst[halves[h]] = v.astype(BF)
+
+        return out
+
+    def direct(src, rec, i0, at, n):
+        def copy(d):
+            v = (i0 + d) % 4
+            return remote(src.at[:, v], rec.at[d - 1], p2s.at[3 * n + d - 1], p2r.at[3 * n + d - 1], at(v))
+
+        def start():
+            for d in (2, 1, 3):
+                go(copy(d))
+
+        def finish():
+            for d in (1, 3, 2):
+                copy(d).wait_recv()
+            return src[:, i0].astype(F32) + rec[0].astype(F32) + rec[1].astype(F32) + rec[2].astype(F32)
+
+        return start, finish
+
+    def spread(src, rec, i0, at, ss, rs, n):
+        def copy(d):
+            v = (i0 + d) % 4
+            return remote(src.at[v], rec.at[d - 1], ss.at[3 * n + d - 1], rs.at[3 * n + d - 1], at(v))
+
+        def start():
+            for d in (2, 1, 3):
+                go(copy(d))
+
+        def finish():
+            for d in (1, 3, 2):
+                copy(d).wait_recv()
+            return (src[i0] + rec[0]) + (rec[1] + rec[2])
+
+        return start, finish
+
+    ring_a, ring_b, dir_a, dir_b, sp_z, sp_h = [], [], [], [], [], []
+    for k in range(2):
+        ica, icb, ra, rb, ia2, ib2, ra2, rb2, iz, rz, ih, rh = parts[k]
+        ring_a.append(
+            reduce_ring(lambda i, h, ic=ica: ic.at[halves[h], :, i], ra, x, at_x, 2 * k, store(ia2))
+        )
+        ring_b.append(
+            reduce_ring(lambda i, h, ic=icb: ic.at[halves[h], i], rb, y, at_y, 2 * k + 1, store(ib2))
+        )
+        dir_a.append(direct(ia2, ra2, y, at_y, 2 * k))
+        dir_b.append(direct(ib2, rb2, x, at_x, 2 * k + 1))
+        sp_z.append(spread(iz, rz, zl, at_z, z2s, z2r, k))
+        sp_h.append(spread(ih, rh, zh, lambda v: at_aux(v * 2 + c), h2s, h2r, k))
+    for k in range(2):
+        integrals_of(k, 0, parts[k][0])
+        ring_a[k][0]()
+        integrals_of(k, 1, parts[k][1])
+        ring_b[k][0]()
+    for k in range(2):
+        ring_a[k][1]()
+        ring_b[k][1]()
+    for k in range(2):
+        ring_a[k][2]()
+        dir_a[k][0]()
+        ring_b[k][2]()
+        dir_b[k][0]()
+    for k in range(2):
+        iz = parts[k][8]
+        iz[:, :, 0:384] = dir_a[k][1]()
+        iz[:, :, 384:768] = dir_b[k][1]()
+        sp_z[k][0]()
+    for k in range(2):
+        tot = sp_z[k][1]()
+        for t in range(4):
+            parts[k][10][t] = tot[:, 192 * t : 192 * t + 192]
+        sp_h[k][0]()
+    integrals = jnp.concatenate([sp_h[k][1]() for k in range(2)], axis=0)
 
     occ0, occ1 = occ_ref[0], occ_ref[1]
     virt = virt_ref[...].reshape(1, 768)
@@ -393,31 +428,20 @@
             pltpu.VMEM((3, 4, 4, 32, 512), BF),
             pltpu.VMEM((3, 4, 2, 32, 512), BF),
             pltpu.VMEM((64, 3, 8, 256), BF),
-            pltpu.VMEM((4, 4, 4, 24, 384), BF),
-            pltpu.VMEM((4, 4, 4, 24, 384), BF),
-            pltpu.VMEM((6, 2, 4, 24, 384), BF),
-            pltpu.VMEM((6, 2, 4, 24, 384), BF),
-            pltpu.VMEM((4, 4, 24, 384), BF),
-            pltpu.VMEM((4, 4, 24, 384), BF),
-            pltpu.VMEM((3, 4, 24, 384), BF),
-            pltpu.VMEM((3, 4, 24, 384), BF),
-            pltpu.VMEM((4, 24, 768), F32),
-            pltpu.VMEM((3, 24, 768), F32),
-            pltpu.VMEM((4, 24, 192), F32),
-            pltpu.VMEM((3, 24, 192), F32),
+            [part_buffers(r) for r in ROWS],
             pltpu.VMEM((16, 8, 128), F32),
             pltpu.VMEM((16, 8, 128), F32),
             pltpu.VMEM((2, 8, 128), F32),
             dma((1,)), dma((3,)),
-            dma((33,)), dma((33,)),
+            dma((30,)), dma((30,)),
             dma((36,)), dma((36,)),
             dma((3,)), dma((3,)),
             dma((3, 4)), dma((3, 4, 4)),
             dma((3, 4)), dma((3, 4)),
+            dma((24,)), dma((24,)),
             dma((12,)), dma((12,)),
             dma((6,)), dma((6,)),
-            dma((3,)), dma((3,)),
-            dma((3,)), dma((3,)),
+            dma((6,)), dma((6,)),
             dma((16,)), dma((16,)),
             dma((16,)), dma((16,)),
             dma((2,)), dma((2,)),

time: 124 us -> 122 us (0.984)
  Pallas kernels: 120 us -> 118 us
    pallas_call x1, Pallas kernels: 120 us -> 118 us  [shards(): pl.pallas_call(kernel, out_shape=(jax.ShapeDtypeStruct((24, 192), F32), j...]
where the time goes in v4:
time: 122 us; the launch traced here: 121 us
  Pallas kernels  118 us (97%)
  between operations  2.4 us (2%)
  local copies, waits for them, and re-layouts  1.35 us (1%)
    pallas_call x1, Pallas kernels, shards(): pl.pallas_call(kernel, out_shape=(jax.ShapeDtypeStruct((24, 192), F32), j...  118 us

profile of v4, /device:TPU:1, one launch (start us, length us, event | category | flops | bytes accessed | tf_op | source)
XLA Modules:
  0.0 121.3 jit_solution(10997617019923212367)
XLA Ops:
  0.6 117.6 %shard_map.59 = (f32[24,192]{1,0:T(8,128)}, f32[1,1]{1,0:T(1,128)}) custom-call(bf16[256,2048]{1,0:T(8,128)(2,1)} %l_hbm.1, bf16[24,2048]{1,0:T(8,128)(2,1)} %bitcast.2, f32[2]{0:T(128)} %occ_ref.1, f32[768]{0:T(1024)} %virt_ref.1), custom_call_target="tpu_custom_call" | custom-call | tf_op jit(solution)/shard_map/pallas_call | solution.py:417
  118.2 1.3 %copy.8 = f32[24,192]{1,0:T(8,128)} copy(f32[24,192]{1,0:T(8,128)} %get-tuple-element.8) | data formatting | bytes 36864

commit v5 on v4

--- a/solution.py
+++ b/solution.py
@@ -9,30 +9,31 @@
 BF = jnp.bfloat16
 F32 = jnp.float32
 NT = (((1,), (1,)), ((), ()))
-ROWS = (16, 8)
-JS = (slice(0, 2), slice(2, 3))
-
-
-def part_buffers(r):
+JS = (slice(0, 2), slice(0, 2), slice(2, 3))
+ROWS = (16, 16, 8)
+CS = ((0, 1), (2,), (0, 1, 2))
+
+
+def part_buffers(r, w):
     return [
-        pltpu.VMEM((4, 4, 4, r, 384), BF),
-        pltpu.VMEM((4, 4, 4, r, 384), BF),
-        pltpu.VMEM((6, 2, 4, r, 384), BF),
-        pltpu.VMEM((6, 2, 4, r, 384), BF),
-        pltpu.VMEM((4, 4, r, 384), BF),
-        pltpu.VMEM((4, 4, r, 384), BF),
-        pltpu.VMEM((3, 4, r, 384), BF),
-        pltpu.VMEM((3, 4, r, 384), BF),
-        pltpu.VMEM((4, r, 768), F32),
-        pltpu.VMEM((3, r, 768), F32),
-        pltpu.VMEM((4, r, 192), F32),
-        pltpu.VMEM((3, r, 192), F32),
+        pltpu.VMEM((4, 4, 4, r, w), BF),
+        pltpu.VMEM((4, 4, 4, r, w), BF),
+        pltpu.VMEM((6, 2, 4, r, w), BF),
+        pltpu.VMEM((6, 2, 4, r, w), BF),
+        pltpu.VMEM((4, 4, r, w), BF),
+        pltpu.VMEM((4, 4, r, w), BF),
+        pltpu.VMEM((3, 4, r, w), BF),
+        pltpu.VMEM((3, 4, r, w), BF),
+        pltpu.VMEM((4, r, 2 * w), F32),
+        pltpu.VMEM((3, r, 2 * w), F32),
+        pltpu.VMEM((4, r, w // 2), F32),
+        pltpu.VMEM((3, r, w // 2), F32),
     ]
 
 
 def kernel(
     l_hbm, b_hbm, occ_ref, virt_ref, amp_ref, en_ref,
-    lv, bt, fp, fx, zs, zr, fo, ftn, parts, ex, ez, ec,
+    lv, bt, fp, fx, zs, zr, fo, ftn, parts, fin, ex, ez, ec,
     lsem, bsem, zss, zrs, ags, agr, cs, cr, hs, hr, xs, xr, rss, rsr, p2s, p2r, z2s, z2r, h2s, h2r,
     exs, exr, ezs, ezr, ecs, ecr,
 ):
@@ -261,19 +262,16 @@
     finish_rows(0)
     finish_home(1)
     finish_rows(1)
-    finish_home(2)
-    finish_rows(2)
-
-    rhs = [
-        jnp.concatenate([ftn[pl.ds((4 * f + 2 * t + c) * 8, 8)].reshape(192, 256) for t in range(2)], axis=0)
-        for f in range(2)
-    ]
-
-    def integrals_of(k, f, ic):
+
+    def integrals_of(k, f):
+        w = 128 * len(CS[k])
+        rhs = jnp.concatenate(
+            [ftn[pl.ds((4 * f + 2 * t + c) * 8, 8), j].reshape(64, 256) for j in CS[k] for t in range(2)], axis=0
+        )
         for z in range(4):
             lhs = ftn[16 * z : 16 * z + 16, JS[k]].reshape(16 * ROWS[k], 256)
-            res = lax.dot_general(lhs, rhs[f], NT, preferred_element_type=F32)
-            ic[z] = res.astype(BF).reshape(4, 4, ROWS[k], 384)
+            res = lax.dot_general(lhs, rhs, NT, preferred_element_type=F32)
+            parts[k][f][z] = res.astype(BF).reshape(4, 4, ROWS[k], w)
 
     def reduce_ring(blk, rec, i0, at, n, out):
         right, left, opp = (i0 + 1) % 4, (i0 + 3) % 4, (i0 + 2) % 4
@@ -344,7 +342,7 @@
         return start, finish
 
     ring_a, ring_b, dir_a, dir_b, sp_z, sp_h = [], [], [], [], [], []
-    for k in range(2):
+    for k in range(3):
         ica, icb, ra, rb, ia2, ib2, ra2, rb2, iz, rz, ih, rh = parts[k]
         ring_a.append(
             reduce_ring(lambda i, h, ic=ica: ic.at[halves[h], :, i], ra, x, at_x, 2 * k, store(ia2))
@@ -356,30 +354,62 @@
         dir_b.append(direct(ib2, rb2, x, at_x, 2 * k + 1))
         sp_z.append(spread(iz, rz, zl, at_z, z2s, z2r, k))
         sp_h.append(spread(ih, rh, zh, lambda v: at_aux(v * 2 + c), h2s, h2r, k))
-    for k in range(2):
-        integrals_of(k, 0, parts[k][0])
+    def begin(k):
+        integrals_of(k, 0)
         ring_a[k][0]()
-        integrals_of(k, 1, parts[k][1])
+        integrals_of(k, 1)
         ring_b[k][0]()
-    for k in range(2):
+
+    def forward(k):
         ring_a[k][1]()
         ring_b[k][1]()
-    for k in range(2):
+
+    def across(k):
         ring_a[k][2]()
         dir_a[k][0]()
         ring_b[k][2]()
         dir_b[k][0]()
-    for k in range(2):
-        iz = parts[k][8]
-        iz[:, :, 0:384] = dir_a[k][1]()
-        iz[:, :, 384:768] = dir_b[k][1]()
+
+    def along_z(k):
+        w = 128 * len(CS[k])
+        parts[k][8][:, :, 0:w] = dir_a[k][1]()
+        parts[k][8][:, :, w : 2 * w] = dir_b[k][1]()
         sp_z[k][0]()
-    for k in range(2):
+
+    def along_z_hi(k):
+        w = 128 * len(CS[k])
         tot = sp_z[k][1]()
-        for t in range(4):
-            parts[k][10][t] = tot[:, 192 * t : 192 * t + 192]
+        for f in range(2):
+            for t in range(2):
+                for n in range(len(CS[k])):
+                    at = f * w + 128 * n + 64 * t
+                    parts[k][10][2 * f + t, :, 64 * n : 64 * n + 64] = tot[:, at : at + 64]
         sp_h[k][0]()
-    integrals = jnp.concatenate([sp_h[k][1]() for k in range(2)], axis=0)
+
+    begin(0)
+    forward(0)
+    finish_home(2)
+    finish_rows(2)
+    begin(1)
+    begin(2)
+    across(0)
+    forward(1)
+    forward(2)
+    along_z(0)
+    across(1)
+    across(2)
+    along_z_hi(0)
+    along_z(1)
+    along_z(2)
+    along_z_hi(1)
+    along_z_hi(2)
+    fin[0:16, 0:128] = sp_h[0][1]()
+    fin[0:16, 128:192] = sp_h[1][1]()
+    fin[16:24, :] = sp_h[2][1]()
+    m = lax.broadcasted_iota(jnp.int32, (192, 192), 0)
+    goal = ((m >> 3) & 7) * 24 + (m >> 6) * 8 + (m & 7)
+    order = (goal == lax.broadcasted_iota(jnp.int32, (192, 192), 1)).astype(F32)
+    integrals = jnp.dot(fin[...], order, precision=lax.Precision.HIGHEST, preferred_element_type=F32)
 
     occ0, occ1 = occ_ref[0], occ_ref[1]
     virt = virt_ref[...].reshape(1, 768)
@@ -428,7 +458,8 @@
             pltpu.VMEM((3, 4, 4, 32, 512), BF),
             pltpu.VMEM((3, 4, 2, 32, 512), BF),
             pltpu.VMEM((64, 3, 8, 256), BF),
-            [part_buffers(r) for r in ROWS],
+            [part_buffers(r, 128 * len(cs)) for r, cs in zip(ROWS, CS)],
+            pltpu.VMEM((24, 192), F32),
             pltpu.VMEM((16, 8, 128), F32),
             pltpu.VMEM((16, 8, 128), F32),
             pltpu.VMEM((2, 8, 128), F32),
@@ -438,10 +469,10 @@
             dma((3,)), dma((3,)),
             dma((3, 4)), dma((3, 4, 4)),
             dma((3, 4)), dma((3, 4)),
-            dma((24,)), dma((24,)),
-            dma((12,)), dma((12,)),
-            dma((6,)), dma((6,)),
-            dma((6,)), dma((6,)),
+            dma((36,)), dma((36,)),
+            dma((18,)), dma((18,)),
+            dma((9,)), dma((9,)),
+            dma((9,)), dma((9,)),
             dma((16,)), dma((16,)),
             dma((16,)), dma((16,)),
             dma((2,)), dma((2,)),
@@ -450,6 +481,17 @@
             collective_id=0, has_side_effects=True, vmem_limit_bytes=56 * 1024 * 1024
         ),
     )(metric_factor, three_centre.T, occ_energy, virt_energy)
+
+    def hand_over(amp_in, en_in, amp_out, en_out):
+        amp_out[...] = amp_in[...]
+        en_out[...] = en_in[...]
+
+    amp, en = pl.pallas_call(
+        hand_over,
+        out_shape=(jax.ShapeDtypeStruct((24, 192), F32), jax.ShapeDtypeStruct((1, 1), F32)),
+        in_specs=[vmem, vmem],
+        out_specs=(vmem, vmem),
+    )(amp, en)
     return amp, en.reshape(())
 
 

time: 122 us -> 116 us (0.951)
  Pallas kernels: 118 us -> 116 us
  between operations: 2.4 us -> 0.64 us
  local copies, waits for them, and re-layouts: 1.35 us -> 0 us
    pallas_call x1, Pallas kernels: 118 us -> 114 us  [shards(): pl.pallas_call(kernel, out_shape=(jax.ShapeDtypeStruct((24, 192), F32), j...]
    pallas_call x0 -> x1, Pallas kernels: none -> 1.96 us  [shards(): pl.pallas_call(hand_over, out_shape=(jax.ShapeDtypeStruct((24, 192), F32)...]
    unnamed x1 -> x0, local copies, waits for them, and re-layouts: 1.35 us -> none
where the time goes in v5:
time: 116 us
  Pallas kernels  116 us (100%)
    pallas_call x1, Pallas kernels, shards(): pl.pallas_call(kernel, out_shape=(jax.ShapeDtypeStruct((24, 192), F32), j...  114 us

profile of v5, /device:TPU:1, one launch (start us, length us, event | category | flops | bytes accessed | tf_op | source)
XLA Modules:
  0.0 116.2 jit_solution(11094935906458769532)
XLA Ops:
  0.6 113.6 %shard_map.59 = (f32[24,192]{1,0:T(8,128)}, f32[1,1]{1,0:T(1,128)}) custom-call(bf16[256,2048]{1,0:T(8,128)(2,1)} %l_hbm.1, bf16[24,2048]{1,0:T(8,128)(2,1)} %bitcast.2, f32[2]{0:T(128)} %occ_ref.1, f32[768]{0:T(1024)} %virt_ref.1), custom_call_target="tpu_custom_call" | custom-call | tf_op jit(solution)/shard_map/pallas_call | solution.py:447
  114.2 2.0 %shard_map.60 = (f32[24,192]{1,0:T(8,128)}, f32[1,1]{1,0:T(1,128)}) custom-call(f32[24,192]{1,0:T(8,128)} %get-tuple-element.6.amp_in, f32[1,1]{1,0:T(1,128)} %get-tuple-element.7.en_in), custom_call_target="tpu_custom_call" | custom-call | tf_op jit(solution)/shard_map/pallas_call | solution.py:489

commit v6 on v5

--- a/solution.py
+++ b/solution.py
@@ -423,7 +423,7 @@
     amp = integrals / (row_gap + col_gap)
     amp_ref[...] = amp
 
-    total = jnp.full((8, 128), jnp.sum(integrals * amp), F32)
+    total = jnp.full((1, 128), jnp.sum(integrals * amp), F32)
     for buf, place, size, at, ss, rs in (
         (ex, y * 4 + x, 16, at_plane, exs, exr),
         (ez, zh * 4 + zl, 16, at_column, ezs, ezr),
@@ -436,7 +436,7 @@
         total = buf[0]
         for i in range(1, size):
             total = total + buf[i]
-    en_ref[...] = -total[0:1, 0:1]
+    en_ref[...] = -total[:, 0:1]
     drain(9)
 
 
@@ -460,9 +460,9 @@
             pltpu.VMEM((64, 3, 8, 256), BF),
             [part_buffers(r, 128 * len(cs)) for r, cs in zip(ROWS, CS)],
             pltpu.VMEM((24, 192), F32),
-            pltpu.VMEM((16, 8, 128), F32),
-            pltpu.VMEM((16, 8, 128), F32),
-            pltpu.VMEM((2, 8, 128), F32),
+            pltpu.VMEM((16, 1, 128), F32),
+            pltpu.VMEM((16, 1, 128), F32),
+            pltpu.VMEM((2, 1, 128), F32),
             dma((1,)), dma((3,)),
             dma((30,)), dma((30,)),
             dma((36,)), dma((36,)),

time: 116 us -> 116 us (level)
  no operation moved by 1% of the time
where the time goes in v6:
time: 116 us
  Pallas kernels  115 us (99%)
    pallas_call x1, Pallas kernels, shards(): pl.pallas_call(kernel, out_shape=(jax.ShapeDtypeStruct((24, 192), F32), j...  113 us

profile of v6, /device:TPU:1, one launch (start us, length us, event | category | flops | bytes accessed | tf_op | source)
XLA Modules:
  0.0 115.6 jit_solution(17982507203795272686)
XLA Ops:
  0.6 113.0 %shard_map.59 = (f32[24,192]{1,0:T(8,128)}, f32[1,1]{1,0:T(1,128)}) custom-call(bf16[256,2048]{1,0:T(8,128)(2,1)} %l_hbm.1, bf16[24,2048]{1,0:T(8,128)(2,1)} %bitcast.2, f32[2]{0:T(128)} %occ_ref.1, f32[768]{0:T(1024)} %virt_ref.1), custom_call_target="tpu_custom_call" | custom-call | tf_op jit(solution)/shard_map/pallas_call | solution.py:447
  113.6 2.0 %shard_map.60 = (f32[24,192]{1,0:T(8,128)}, f32[1,1]{1,0:T(1,128)}) custom-call(f32[24,192]{1,0:T(8,128)} %get-tuple-element.6.amp_in, f32[1,1]{1,0:T(1,128)} %get-tuple-element.7.en_in), custom_call_target="tpu_custom_call" | custom-call | tf_op jit(solution)/shard_map/pallas_call | solution.py:489

commit v7 on v6

--- a/solution.py
+++ b/solution.py
@@ -12,6 +12,10 @@
 JS = (slice(0, 2), slice(0, 2), slice(2, 3))
 ROWS = (16, 16, 8)
 CS = ((0, 1), (2,), (0, 1, 2))
+
+
+COLUMN = sorted(range(1, 16), key=lambda d: -min(d, 16 - d))
+PLANE = sorted(range(1, 16), key=lambda d: -(min(d % 4, 4 - d % 4) + min(d // 4, 4 - d // 4)))
 
 
 def part_buffers(r, w):
@@ -106,9 +110,10 @@
                     to_other(j, q).wait_send()
 
     barrier = pltpu.get_barrier_semaphore()
-    for d in range(1, 16):
+    for d in COLUMN:
+        pl.semaphore_signal(barrier, inc=1, device_id=at_column(d), device_id_type=MESH)
+    for d in PLANE:
         pl.semaphore_signal(barrier, inc=1, device_id=at_plane(d), device_id_type=MESH)
-        pl.semaphore_signal(barrier, inc=1, device_id=at_column(d), device_id_type=MESH)
     pl.semaphore_signal(barrier, inc=1, device_id=other, device_id_type=MESH)
     own = []
     for j in range(3):
@@ -424,13 +429,13 @@
     amp_ref[...] = amp
 
     total = jnp.full((1, 128), jnp.sum(integrals * amp), F32)
-    for buf, place, size, at, ss, rs in (
-        (ex, y * 4 + x, 16, at_plane, exs, exr),
-        (ez, zh * 4 + zl, 16, at_column, ezs, ezr),
-        (ec, c, 2, lambda d: other, ecs, ecr),
+    for buf, place, size, away, at, ss, rs in (
+        (ex, y * 4 + x, 16, PLANE, at_plane, exs, exr),
+        (ez, zh * 4 + zl, 16, COLUMN, at_column, ezs, ezr),
+        (ec, c, 2, (1,), lambda d: other, ecs, ecr),
     ):
         buf[place] = total
-        waits = [go(remote(buf.at[place], buf.at[place], ss.at[d], rs.at[d], at(d))) for d in range(1, size)]
+        waits = [go(remote(buf.at[place], buf.at[place], ss.at[d], rs.at[d], at(d))) for d in away]
         for w in waits:
             w.wait_recv()
         total = buf[0]

time: 116 us -> 115 us (level)
  no operation moved by 1% of the time
where the time goes in v7:
time: 115 us
  Pallas kernels  114 us (99%)
    pallas_call x1, Pallas kernels, shards(): pl.pallas_call(kernel, out_shape=(jax.ShapeDtypeStruct((24, 192), F32), j...  113 us

profile of v7, /device:TPU:1, one launch (start us, length us, event | category | flops | bytes accessed | tf_op | source)
XLA Modules:
  0.0 115.1 jit_solution(2438177260636304624)
XLA Ops:
  0.6 112.5 %shard_map.59 = (f32[24,192]{1,0:T(8,128)}, f32[1,1]{1,0:T(1,128)}) custom-call(bf16[256,2048]{1,0:T(8,128)(2,1)} %l_hbm.1, bf16[24,2048]{1,0:T(8,128)(2,1)} %bitcast.2, f32[2]{0:T(128)} %occ_ref.1, f32[768]{0:T(1024)} %virt_ref.1), custom_call_target="tpu_custom_call" | custom-call | tf_op jit(solution)/shard_map/pallas_call | solution.py:452
  113.2 2.0 %shard_map.60 = (f32[24,192]{1,0:T(8,128)}, f32[1,1]{1,0:T(1,128)}) custom-call(f32[24,192]{1,0:T(8,128)} %get-tuple-element.6.amp_in, f32[1,1]{1,0:T(1,128)} %get-tuple-element.7.en_in), custom_call_target="tpu_custom_call" | custom-call | tf_op jit(solution)/shard_map/pallas_call | solution.py:494
